TPU v7x, 32 devices: a whole 2x2x4 slice. The times are simulated.
32 devices in a mesh: col: 4 (over z), row: 8 (over y, x, core).
Axes of the slice: x: 2, y: 2, z: 4, core: 2. Of those that a mesh axis runs over, the one named last changes fastest.
Arguments:
- affinity: bfloat16 [3840, 128, 128], P(('col', 'row')), may hold values from 0 to 0.015625
- tile_rows: int32 [3840], P(('col', 'row')), may hold values from 0 to 19
- tile_cols: int32 [3840], P(('col', 'row')), may hold values from 0 to 39
- live_tiles: int32 [32], P(('col', 'row')), may hold values from 1 to 120, as said below
- start: float32 [20480, 256], P(('col', 'row')), may hold values from -1500 to 1500
Outputs:
- vectors: float32 [20480, 256], P(('col', 'row'))
- first_passes: float32 [2, 20480, 256], P(None, ('col', 'row'))
Inputs may be any that keep to these rules, and one draw needn't show every extreme that they name: A device's tiles are its slots 0 to live_tiles - 1; later slots are ignored. Some device holds exactly 120 tiles.
All inputs are finite; a program needn't handle non-finite values.
Results may differ from a plain program's by a relative error of at most 0.0003.
Values sent between devices are 32-bit elements; how exact they have to be, the bound alone decides.
No kernel may reach another device: no remote copies, remote signals or barrier semaphores. Data moves between devices by JAX's collectives and lax.ppermute only.
A program may use at most 128 MiB of HBM per device.

v0:
```python
import jax
import jax.numpy as jnp
from jax import lax
from jax.sharding import PartitionSpec as P

ITERS = 2
highest = lax.Precision.HIGHEST


def local_gram(matrix):
    return jnp.dot(matrix.T, matrix, precision=highest, preferred_element_type=jnp.float32)


def inverse_lower(gram):
    lower = jnp.linalg.cholesky(gram)
    return jax.scipy.linalg.solve_triangular(
        lower, jnp.eye(gram.shape[0], dtype=jnp.float32), lower=True
    )


def apply_factor(matrix, inverse):
    return jnp.dot(matrix, inverse.T, precision=highest, preferred_element_type=jnp.float32)


def body(affinity, tile_rows, tile_cols, live_tiles, start):
    n_row = lax.axis_size("row")
    n_col = lax.axis_size("col")
    slot_count = affinity.shape[0]
    tile_size = affinity.shape[1]
    rows_local = start.shape[0]
    vec_count = start.shape[1]
    own_tiles = rows_local // tile_size
    live = (jnp.arange(slot_count) < live_tiles[0]).astype(jnp.float32)
    row_onehot = (jnp.arange(own_tiles * n_col)[:, None] == tile_rows[None, :]).astype(
        jnp.float32
    ) * live[None, :]
    row_sums = jnp.sum(affinity, axis=2, dtype=jnp.float32)
    degree_terms = jnp.dot(
        row_onehot, row_sums, precision=highest, preferred_element_type=jnp.float32
    )
    degree = 1.0 + lax.psum_scatter(degree_terms, "col", scatter_dimension=0, tiled=True).reshape(
        rows_local
    )
    scaling = (1.0 / jnp.sqrt(degree))[:, None]
    squares = affinity.astype(jnp.float32)
    firsts = []
    pending = start
    for step_number in range(ITERS):
        mapped_scaled = scaling * pending
        gathered = lax.all_gather(mapped_scaled, "row", axis=0, tiled=True)
        gathered = gathered.reshape(n_row * own_tiles, tile_size, vec_count)
        picked = gathered[tile_cols]
        products = jnp.einsum(
            "sij,sjk->sik", squares, picked, precision=highest, preferred_element_type=jnp.float32
        )
        terms = jnp.dot(
            row_onehot,
            products.reshape(slot_count, tile_size * vec_count),
            precision=highest,
            preferred_element_type=jnp.float32,
        )
        summed = lax.psum_scatter(terms, "col", scatter_dimension=0, tiled=True)
        raw_image = scaling * (mapped_scaled + summed.reshape(rows_local, vec_count))
        if step_number == 0:
            inner_gram = lax.psum(local_gram(raw_image), ("col", "row"))
            image_block = raw_image
        else:
            raw_gram, pending_gram = lax.psum(
                (local_gram(raw_image), local_gram(pending)), ("col", "row")
            )
            pending_inverse = inverse_lower(pending_gram)
            image_block = apply_factor(raw_image, pending_inverse)
            inner_gram = jnp.dot(
                jnp.dot(
                    pending_inverse, raw_gram, precision=highest, preferred_element_type=jnp.float32
                ),
                pending_inverse.T,
                precision=highest,
                preferred_element_type=jnp.float32,
            )
        pending = apply_factor(image_block, inverse_lower(inner_gram))
        firsts.append(pending)
    final_gram = lax.psum(local_gram(pending), ("col", "row"))
    basis = apply_factor(pending, inverse_lower(final_gram))
    total_images = rows_local * n_row * n_col
    root = jnp.sqrt(jnp.float32(total_images))
    return (root * basis, root * jnp.stack(firsts, axis=0))


def solution(mesh):
    placed = (
        P(("col", "row"), None, None),
        P(("col", "row")),
        P(("col", "row")),
        P(("col", "row")),
        P(("col", "row"), None),
    )
    return jax.shard_map(
        body,
        mesh=mesh,
        in_specs=placed,
        out_specs=(P(("col", "row"), None), P(None, ("col", "row"), None)),
        check_vma=False,
    )
```

profile of v0, /device:TPU:0, one launch (start us, length us, event | category | flops | bytes accessed | tf_op | source)
XLA Modules:
  0.0 1157.0 jit_solution(773065271221598994)
XLA Ops:
  7.9 3.2 convert_reduce_fusion
  11.9 20.4 %all-reduce.1 = f32[20,128]{1,0:T(8,128)S(1)} all-reduce(f32[20,128]{1,0:T(8,128)S(1)} %fusion.55), channel_id=2, replica_groups=mesh['col'=4,'row'=8] {'col'}, use_global_device_ids=true, to_apply=%region_1.0.clone | all-reduce | flops 2560 | bytes 20480
  32.4 1.4 fusion.81
  34.4 2.1 broadcast_multiply_fusion.1
  36.6 39.3 %all-gather.3.cloned.1.call-done = f32[5120,256]{1,0:T(8,128)} async-done(((f32[640,256]{1,0:T(8,128)}), f32[5120,256]{1,0:T(8,128)}) %all-gather.3.cloned.1.call-update) | async-done | bytes 5242896 | tf_op jit(solution)/shard_map/all_gather | solution.py:50
  75.9 12.1 %gather_fusion = f32[120,128,256]{2,1,0:T(8,128)} fusion(f32[40,128,256]{2,1,0:T(8,128)} %bitcast.166, s32[1024]{0:T(1024)S(1)} %pad_clamp_fusion), kind=kCustom, calls=%fused_computation | custom fusion | bytes 31457760 | tf_op jit(solution)/shard_map/gather | solution.py:52
  88.0 20.2 %convolution_bitcast_fusion.1 = f32[120,128,256]{1,2,0:T(8,128)} fusion(f32[120,128,256]{2,1,0:T(8,128)} %gather_fusion, bf16[120,128,128]{2,1,0:T(8,128)(2,1)} %param.8), kind=kOutput, calls=%fused_computation.11 | convolution fusion | flops 6039797760 | bytes 35389440 | tf_op jit(solution)/shard_map/sij,sjk->sik/dot_general | solution.py:53
  108.2 15.7 %copy.41 = f32[15,8,128,256]{3,1,2,0:T(8,128)} copy(f32[15,8,128,256]{2,3,1,0:T(8,128)} %bitcast.163) | data formatting | bytes 31457280
  123.9 10.5 fusion.53
  134.4 78.5 %fusion = f32[8,32768]{1,0:T(8,128)} fusion(f32[20,32768]{1,0:T(8,128)S(1)} %fusion.53), kind=kCustom, calls=%all-reduce-scatter | all-reduce-scatter fusion | flops 1048577 | bytes 3670528
  212.9 1.5 collective-permute-start
  214.4 1.3 slice.54
  215.7 2.6 collective-permute-start.1
  219.0 20.1 %collective-permute-done.1 = f32[1,32768]{1,0:T(1,128)S(1)} collective-permute-done((f32[1,32768]{1,0:T(1,128)S(1)}, f32[1,32768]{1,0:T(1,128)S(1)}, u32[]{:S(2)}, u32[]{:S(2)}) %collective-permute-start.1) | collective-permute-done | bytes 131104
  239.1 21.2 %concatenate.3 = f32[17,32768]{1,0:T(8,128)} concatenate(f32[1,32768]{1,0:T(1,128)S(1)} %collective-permute-done.1, f32[8,32768]{1,0:T(8,128)S(1)} %collective-permute-done, f32[8,32768]{1,0:T(8,128)} %fusion), dimensions={0} | concatenate | bytes 4456448
  260.3 1.7 constant_dynamic-slice_fusion.5
  262.4 2.2 fusion.29
  264.6 129.0 %all-reduce.11.cloned.1.call-done = f32[256,256]{0,1:T(8,128)} async-done(((f32[256,256]{0,1:T(8,128)}), f32[256,256]{0,1:T(8,128)}) %all-reduce.11.cloned.1.call-update) | async-done | bytes 262160 | tf_op jit(solution)/shard_map/psum | solution.py:65
  395.7 11.7 %cholesky.214 = f32[128,128]{1,0:T(8,128)S(1)} custom-call(f32[128,128]{1,0:T(8,128)S(1)} %cholesky.346), custom_call_target="Cholesky" | custom-call | tf_op jit(solution)/shard_map/jit(cholesky)/cholesky | solution.py:15
  407.5 9.8 custom-call.17
  417.8 11.7 %cholesky.231 = f32[128,128]{1,0:T(8,128)S(1)} custom-call(f32[128,128]{1,0:T(8,128)S(1)} %convolution_subtract_fusion.7), custom_call_target="Cholesky" | custom-call | tf_op jit(solution)/shard_map/jit(cholesky)/cholesky | solution.py:15
  431.8 15.1 %while.8 = (s32[]{:T(128)}, f32[256,256]{1,0:T(8,128)S(1)}, s32[2,2]{1,0:T(2,128)S(1)}, f32[2,128,128]{2,1,0:T(8,128)S(1)}, s32[]{:T(128)}) while((s32[]{:T(128)}, f32[256,256]{1,0:T(8,128)S(1)}, s32[2,2]{1,0:T(2,128)S(1)}, f32[2,128,128]{2,1,0:T(8,128)S(1)}, s32[]{:T(128)}) %tuple.83), condition=%wide.while_cond, body=%wide.while_body.sunk | while | flops 2 | bytes 131181 | solution.py:16
  443.4 1.4 bitcast_dynamic-update-slice_fusion.8
  445.5 1.4 bitcast_dynamic-update-slice_fusion.8
  446.9 19.7 %custom-call.18 = f32[2,128,128]{1,2,0:T(8,128)S(1)} custom-call(f32[2,128,128]{2,1,0:T(8,128)S(1)} %get-tuple-element.30), custom_call_target="InvertDiagBlocksLowerTriangular" | custom-call | tf_op jit(solution)/shard_map/jit(_solve_triangular)/triangular_solve | solution.py:16
  467.5 1.6 broadcast_multiply_fusion
  469.1 40.2 %all-gather.5.cloned.1.call-done = f32[5120,256]{1,0:T(8,128)} async-done(((f32[640,256]{1,0:T(8,128)}), f32[5120,256]{1,0:T(8,128)}) %all-gather.5.cloned.1.call-update) | async-done | bytes 5242896 | tf_op jit(solution)/shard_map/all_gather | solution.py:50
  509.3 12.1 %gather_fusion.1 = f32[120,128,256]{2,1,0:T(8,128)} fusion(f32[40,128,256]{2,1,0:T(8,128)} %bitcast.167, s32[1024]{0:T(1024)S(1)} %pad_clamp_fusion), kind=kCustom, calls=%fused_computation.1 | custom fusion | bytes 31457760 | tf_op jit(solution)/shard_map/gather | solution.py:52
  521.4 20.2 %convolution_bitcast_fusion = f32[120,128,256]{1,2,0:T(8,128)} fusion(f32[120,128,256]{2,1,0:T(8,128)} %gather_fusion.1, bf16[120,128,128]{2,1,0:T(8,128)(2,1)} %param.8), kind=kOutput, calls=%fused_computation.10 | convolution fusion | flops 6039797760 | bytes 35389440 | tf_op jit(solution)/shard_map/sij,sjk->sik/dot_general | solution.py:53
  541.6 15.7 %copy.42 = f32[15,8,128,256]{3,1,2,0:T(8,128)} copy(f32[15,8,128,256]{2,3,1,0:T(8,128)} %bitcast.165) | data formatting | bytes 31457280
  557.3 11.6 fusion.51
  568.9 78.6 %fusion.1 = f32[8,32768]{1,0:T(8,128)S(1)} fusion(f32[20,32768]{1,0:T(8,128)} %fusion.51), kind=kCustom, calls=%all-reduce-scatter.1 | all-reduce-scatter fusion | flops 1048577 | bytes 3670528
  647.4 2.3 collective-permute-start.2
  649.8 1.7 collective-permute-start.3
  651.5 1.9 fusion.82
  653.4 19.9 %collective-permute-done.3 = f32[1,32768]{1,0:T(1,128)S(1)} collective-permute-done((f32[1,32768]{1,0:T(1,128)S(1)}, f32[1,32768]{1,0:T(1,128)S(1)}, u32[]{:S(2)}, u32[]{:S(2)}) %collective-permute-start.3) | collective-permute-done | bytes 131104
  673.3 21.2 %concatenate.4 = f32[17,32768]{1,0:T(8,128)} concatenate(f32[1,32768]{1,0:T(1,128)S(1)} %collective-permute-done.3, f32[8,32768]{1,0:T(8,128)} %collective-permute-done.2, f32[8,32768]{1,0:T(8,128)S(1)} %fusion.1), dimensions={0} | concatenate | bytes 4456448
  694.5 1.7 constant_dynamic-slice_fusion.4
  696.6 2.1 fusion.30
  698.8 131.3 %all-reduce.15.cloned.1.call-done = (f32[256,256]{0,1:T(8,128)}, f32[256,256]{1,0:T(8,128)}) async-done(((f32[256,256]{0,1:T(8,128)}, f32[256,256]{1,0:T(8,128)}), (f32[256,256]{0,1:T(8,128)}, f32[256,256]{1,0:T(8,128)})) %all-reduce.15.cloned.1.call-update) | async-done | bytes 524304 | tf_op jit(solution)/shard_map/psum | solution.py:68
  832.2 11.7 %cholesky.248 = f32[128,128]{1,0:T(8,128)S(1)} custom-call(f32[128,128]{1,0:T(8,128)S(1)} %cholesky.349), custom_call_target="Cholesky" | custom-call | tf_op jit(solution)/shard_map/jit(cholesky)/cholesky | solution.py:15
  844.0 9.8 custom-call.19
  854.3 11.7 %cholesky.265 = f32[128,128]{1,0:T(8,128)S(1)} custom-call(f32[128,128]{1,0:T(8,128)S(1)} %convolution_subtract_fusion.6), custom_call_target="Cholesky" | custom-call | tf_op jit(solution)/shard_map/jit(cholesky)/cholesky | solution.py:15
  868.7 4.0 while.9
  869.3 1.4 bitcast_dynamic-update-slice_fusion.9
  871.3 1.4 bitcast_dynamic-update-slice_fusion.9
  872.7 19.8 %custom-call.20 = f32[2,128,128]{1,2,0:T(8,128)S(1)} custom-call(f32[2,128,128]{2,1,0:T(8,128)S(1)} %get-tuple-element.31), custom_call_target="InvertDiagBlocksLowerTriangular" | custom-call | tf_op jit(solution)/shard_map/jit(_solve_triangular)/triangular_solve | solution.py:16
  895.2 11.7 %cholesky.282 = f32[128,128]{1,0:T(8,128)S(1)} custom-call(f32[128,128]{1,0:T(8,128)S(1)} %cholesky.352), custom_call_target="Cholesky" | custom-call | tf_op jit(solution)/shard_map/jit(cholesky)/cholesky | solution.py:15
  907.0 9.8 custom-call.21
  917.3 11.9 %cholesky.299 = f32[128,128]{1,0:T(8,128)S(1)} custom-call(f32[128,128]{1,0:T(8,128)S(1)} %convolution_subtract_fusion.5), custom_call_target="Cholesky" | custom-call | tf_op jit(solution)/shard_map/jit(cholesky)/cholesky | solution.py:15
  931.8 4.0 while.10
  932.4 1.4 bitcast_dynamic-update-slice_fusion.10
  934.5 1.4 bitcast_dynamic-update-slice_fusion.10
  935.8 19.7 %custom-call.22 = f32[2,128,128]{1,2,0:T(8,128)S(1)} custom-call(f32[2,128,128]{2,1,0:T(8,128)S(1)} %get-tuple-element.32), custom_call_target="InvertDiagBlocksLowerTriangular" | custom-call | tf_op jit(solution)/shard_map/jit(_solve_triangular)/triangular_solve | solution.py:16
  957.2 1.9 fusion.83
  960.3 124.6 %all-reduce.13.cloned.1.call-done = f32[256,256]{0,1:T(8,128)} async-done(((f32[256,256]{0,1:T(8,128)}), f32[256,256]{0,1:T(8,128)}) %all-reduce.13.cloned.1.call-update) | async-done | bytes 262160 | tf_op jit(solution)/shard_map/psum | solution.py:83
  1087.0 11.7 %cholesky.316 = f32[128,128]{1,0:T(8,128)S(1)} custom-call(f32[128,128]{1,0:T(8,128)S(1)} %cholesky.355), custom_call_target="Cholesky" | custom-call | tf_op jit(solution)/shard_map/jit(cholesky)/cholesky | solution.py:15
  1098.8 9.8 custom-call.23
  1109.1 11.9 %cholesky.333 = f32[128,128]{1,0:T(8,128)S(1)} custom-call(f32[128,128]{1,0:T(8,128)S(1)} %convolution_subtract_fusion.4), custom_call_target="Cholesky" | custom-call | tf_op jit(solution)/shard_map/jit(cholesky)/cholesky | solution.py:15
  1123.8 4.1 while.11
  1124.4 1.4 bitcast_dynamic-update-slice_fusion.11
  1126.5 1.4 bitcast_dynamic-update-slice_fusion.11
  1127.9 19.7 %custom-call.24 = f32[2,128,128]{1,2,0:T(8,128)S(1)} custom-call(f32[2,128,128]{2,1,0:T(8,128)S(1)} %get-tuple-element.33), custom_call_target="InvertDiagBlocksLowerTriangular" | custom-call | tf_op jit(solution)/shard_map/jit(_solve_triangular)/triangular_solve | solution.py:16
  1148.5 1.6 convolution_multiply_fusion
  (111 shorter events, 27.2 us)
Async XLA Ops:
  7.2 29.4 %copy-start.3 = (s32[120]{0:T(128)S(1)}, s32[120]{0:T(128)}, u32[]{:S(2)}) copy-start(s32[120]{0:T(128)} %param.10) | copy-start | bytes 1444
  7.2 68.7 %all-gather.3.cloned.1.call-start = ((), (), s32[]{:S(2)}) async-start(), calls=%async_computation | async-start | bytes 5898240 | tf_op jit(solution)/shard_map/all_gather | solution.py:50
  36.5 357.1 %all-reduce.11.cloned.1.call-start = ((), (), s32[]{:S(2)}) async-start(), calls=%async_computation.1 | async-start | bytes 524288 | tf_op jit(solution)/shard_map/psum | solution.py:65
  108.2 15.7 %copy-start.2 = (s32[120]{0:T(128)S(1)}, s32[120]{0:T(128)}, u32[]{:S(2)}) copy-start(s32[120]{0:T(128)} %param.9) | copy-start | bytes 1444
  212.9 49.5 %copy-start = (f32[640,256]{1,0:T(8,128)S(1)}, f32[640,256]{1,0:T(8,128)}, u32[]{:S(2)}) copy-start(f32[640,256]{1,0:T(8,128)} %param.12) | copy-start | bytes 1966084
  212.9 26.2 %collective-permute-start = (f32[8,32768]{1,0:T(8,128)}, f32[8,32768]{1,0:T(8,128)S(1)}, u32[]{:S(2)}, u32[]{:S(2)}) collective-permute-start(f32[8,32768]{1,0:T(8,128)} %fusion), channel_id=1, source_target_pairs={{0,8},{8,16},{16,24},{1,9},{9,17},{17,25},{2,10},{10,18},{18,26},{... | collective-permute-start | bytes 3145736
  215.7 23.4 %collective-permute-start.1 = (f32[1,32768]{1,0:T(1,128)S(1)}, f32[1,32768]{1,0:T(1,128)S(1)}, u32[]{:S(2)}, u32[]{:S(2)}) collective-permute-start(f32[1,32768]{1,0:T(1,128)S(1)} %slice.54), channel_id=1, source_target_pairs={{0,16},{8,24},{1,17},{9,25},{2,18},{10,26},{3,19},{11,27},{4,20},{... | collective-permute-start | bytes 393224
  264.6 244.7 %all-gather.5.cloned.1.call-start = ((), (), s32[]{:S(2)}) async-start(), calls=%async_computation.2 | async-start | bytes 5898240 | tf_op jit(solution)/shard_map/all_gather | solution.py:50
  469.1 361.0 %all-reduce.15.cloned.1.call-start = ((), (), s32[]{:S(2)}) async-start(), calls=%async_computation.4 | async-start | bytes 1048576 | tf_op jit(solution)/shard_map/psum | solution.py:68
  647.4 25.9 %collective-permute-start.2 = (f32[8,32768]{1,0:T(8,128)S(1)}, f32[8,32768]{1,0:T(8,128)}, u32[]{:S(2)}, u32[]{:S(2)}) collective-permute-start(f32[8,32768]{1,0:T(8,128)S(1)} %fusion.1), channel_id=1, source_target_pairs={{0,8},{8,16},{16,24},{1,9},{9,17},{17,25},{2,10},{10,18},{18,26},{... | collective-permute-start | bytes 3145736
  649.8 23.5 %collective-permute-start.3 = (f32[1,32768]{1,0:T(1,128)S(1)}, f32[1,32768]{1,0:T(1,128)S(1)}, u32[]{:S(2)}, u32[]{:S(2)}) collective-permute-start(f32[1,32768]{1,0:T(1,128)S(1)} %slice.55), channel_id=1, source_target_pairs={{0,16},{8,24},{1,17},{9,25},{2,18},{10,26},{3,19},{11,27},{4,20},{... | collective-permute-start | bytes 393224
  698.7 386.2 %all-reduce.13.cloned.1.call-start = ((), (), s32[]{:S(2)}) async-start(), calls=%async_computation.3 | async-start | bytes 524288 | tf_op jit(solution)/shard_map/psum | solution.py:83
  830.1 64.1 %copy-start.1 = (f32[256,256]{1,0:T(8,128)S(1)}, f32[256,256]{1,0:T(8,128)}, u32[]{:S(2)}) copy-start(f32[256,256]{1,0:T(8,128)} %get-tuple-element.67) | copy-start | bytes 786436
Sparse Core Ops, SparseCore 0:
  36.7 39.1 all-gather.2
  264.7 128.9 all-reduce.10
  469.2 40.0 all-gather.4
  698.9 131.1 all-reduce.14
  959.2 125.6 all-reduce.12
where the time goes:
time: 1170 us; the launch traced here: 1160 us
  waiting for transfers between devices  504 us (43%)
  other arithmetic  227 us (19%)
  blocking collectives  177 us (15%)
  local copies, waits for them, and re-layouts  125 us (11%)
  matrix products  82.1 us (7%)
  between operations  22.1 us (2%)
    unnamed x3, blocking collectives  177 us
    another operation x27, other arithmetic, inverse_lower(): lower = jnp.linalg.cholesky(gram)  138 us
    psum x1, waiting for transfers between devices, body(): lax.psum((local_gram(raw_image), local_gram(pending)), ('col', 'row'))  131 us
    psum x1, waiting for transfers between devices, body(): inner_gram = lax.psum(local_gram(raw_image), ('col', 'row'))  129 us
    psum x1, waiting for transfers between devices, body(): final_gram = lax.psum(local_gram(pending), ('col', 'row'))  125 us
    unnamed x17, local copies, waits for them, and re-layouts  80.2 us
    all_gather x2, waiting for transfers between devices, body(): gathered = lax.all_gather(mapped_scaled, 'row', axis=0, tiled=True)  79.4 us
    another operation x9, other arithmetic, inverse_lower(): jax.scipy.linalg.solve_triangular(lower, jnp.eye(gram.shape[0], dtype=jnp...  79 us
  transfers between devices with their start and end apart: 9, of which 7 were waited for; matrix products, arithmetic and copies ran while one was open for 0% of the time, Pallas kernels for 0%

commit v1 on v0

--- a/solution.py
+++ b/solution.py
@@ -47,7 +47,9 @@
     pending = start
     for step_number in range(ITERS):
         mapped_scaled = scaling * pending
-        gathered = lax.all_gather(mapped_scaled, "row", axis=0, tiled=True)
+        gathered = jnp.concatenate(
+            lax.all_to_all(jnp.stack([mapped_scaled] * lax.axis_size("row")), "row", 0, 0), axis=0
+        )
         gathered = gathered.reshape(n_row * own_tiles, tile_size, vec_count)
         picked = gathered[tile_cols]
         products = jnp.einsum(

time: 1170 us -> 1200 us (1.026)
  blocking collectives: 177 us -> 233 us
  waiting for transfers between devices: 504 us -> 488 us
    all_gather x2 -> x0, waiting for transfers between devices: 79.4 us -> none  [body(): gathered = lax.all_gather(mapped_scaled, 'row', axis=0, tiled=True)]
    all_to_all x0 -> x1, blocking collectives: none -> 63.8 us  [body(): lax.all_to_all(jnp.stack([mapped_scaled] * lax.axis_size('row')), 'row',...]
    all_to_all x0 -> x1, waiting for transfers between devices: none -> 60.1 us  [body(): lax.all_to_all(jnp.stack([mapped_scaled] * lax.axis_size('row')), 'row',...]
    unnamed x9 -> x7, waiting for transfers between devices: 40 us -> 36.2 us
  transfers between devices with their start and end apart: 9 -> 8, of which waited for: 7 -> 6; matrix products, arithmetic and copies ran while one was open for 0% -> 0% of each run, Pallas kernels for 0% -> 0%
where the time goes in v1:
time: 1200 us; the launch traced here: 1190 us
  waiting for transfers between devices  488 us (41%)
  blocking collectives  233 us (19%)
  other arithmetic  226 us (19%)
  local copies, waits for them, and re-layouts  128 us (11%)
  matrix products  81.3 us (7%)
  between operations  21.9 us (2%)
  starting transfers between devices  13.8 us (1%)
    unnamed x3, blocking collectives  169 us
    another operation x27, other arithmetic, inverse_lower(): lower = jnp.linalg.cholesky(gram)  138 us
    psum x1, waiting for transfers between devices, body(): inner_gram = lax.psum(local_gram(raw_image), ('col', 'row'))  135 us
    psum x1, waiting for transfers between devices, body(): lax.psum((local_gram(raw_image), local_gram(pending)), ('col', 'row'))  133 us
    psum x1, waiting for transfers between devices, body(): final_gram = lax.psum(local_gram(pending), ('col', 'row'))  125 us
    unnamed x17, local copies, waits for them, and re-layouts  80.1 us
    another operation x9, other arithmetic, inverse_lower(): jax.scipy.linalg.solve_triangular(lower, jnp.eye(gram.shape[0], dtype=jnp...  79 us
    all_to_all x1, blocking collectives, body(): lax.all_to_all(jnp.stack([mapped_scaled] * lax.axis_size('row')), 'row',...  63.8 us
  transfers between devices with their start and end apart: 8, of which 6 were waited for; matrix products, arithmetic and copies ran while one was open for 0% of the time, Pallas kernels for 0%

profile of v1, /device:TPU:0, one launch (start us, length us, event | category | flops | bytes accessed | tf_op | source)
XLA Modules:
  0.0 1192.6 jit_solution(5159537698940306170)
XLA Ops:
  7.8 3.2 convert_reduce_fusion
  11.9 20.4 %all-reduce.1 = f32[20,128]{1,0:T(8,128)S(1)} all-reduce(f32[20,128]{1,0:T(8,128)S(1)} %fusion.55), channel_id=2, replica_groups=mesh['col'=4,'row'=8] {'col'}, use_global_device_ids=true, to_apply=%region_1.0.clone | all-reduce | flops 2560 | bytes 20480
  32.3 1.3 fusion.81
  35.5 2.8 stack.10
  38.3 4.8 all-to-all-start
  43.3 60.1 %all-to-all-done = f32[8,640,256]{2,1,0:T(8,128)} async-done(((f32[8,640,256]{2,1,0:T(8,128)}), f32[8,640,256]{2,1,0:T(8,128)}, u32[]{:S(2)}, u32[]{:S(2)}) %all-to-all-start) | async-done | bytes 5242912 | tf_op jit(solution)/shard_map/all_to_all | solution.py:51
  103.4 12.1 %gather_fusion = f32[120,128,256]{2,1,0:T(8,128)} fusion(f32[40,128,256]{2,1,0:T(8,128)} %bitcast.2, s32[1024]{0:T(1024)S(1)} %pad_clamp_fusion), kind=kCustom, calls=%fused_computation | custom fusion | bytes 31457760 | tf_op jit(solution)/shard_map/gather | solution.py:54
  115.6 20.2 %convolution_bitcast_fusion.1 = f32[120,128,256]{1,2,0:T(8,128)} fusion(f32[120,128,256]{2,1,0:T(8,128)} %gather_fusion, bf16[120,128,128]{2,1,0:T(8,128)(2,1)} %param.8), kind=kOutput, calls=%fused_computation.11 | convolution fusion | flops 6039797760 | bytes 35389440 | tf_op jit(solution)/shard_map/sij,sjk->sik/dot_general | solution.py:55
  135.7 15.7 %copy.41 = f32[15,8,128,256]{3,1,2,0:T(8,128)} copy(f32[15,8,128,256]{2,3,1,0:T(8,128)} %bitcast.164) | data formatting | bytes 31457280
  151.5 10.5 fusion.53
  161.9 72.8 %fusion = f32[8,32768]{1,0:T(8,128)} fusion(f32[20,32768]{1,0:T(8,128)S(1)} %fusion.53), kind=kCustom, calls=%all-reduce-scatter | all-reduce-scatter fusion | flops 1048577 | bytes 3670528
  234.8 1.5 collective-permute-start
  236.2 1.3 slice.54
  237.6 2.6 collective-permute-start.1
  240.8 17.3 %collective-permute-done.1 = f32[1,32768]{1,0:T(1,128)S(1)} collective-permute-done((f32[1,32768]{1,0:T(1,128)S(1)}, f32[1,32768]{1,0:T(1,128)S(1)}, u32[]{:S(2)}, u32[]{:S(2)}) %collective-permute-start.1) | collective-permute-done | bytes 131104
  258.1 21.2 %concatenate.3 = f32[17,32768]{1,0:T(8,128)} concatenate(f32[1,32768]{1,0:T(1,128)S(1)} %collective-permute-done.1, f32[8,32768]{1,0:T(8,128)S(1)} %collective-permute-done, f32[8,32768]{1,0:T(8,128)} %fusion), dimensions={0} | concatenate | bytes 4456448
  279.3 1.7 constant_dynamic-slice_fusion.5
  281.4 2.2 fusion.29
  283.6 134.5 %all-reduce.11.cloned.1.call-done = f32[256,256]{0,1:T(8,128)} async-done(((f32[256,256]{0,1:T(8,128)}), f32[256,256]{0,1:T(8,128)}) %all-reduce.11.cloned.1.call-update) | async-done | bytes 262160 | tf_op jit(solution)/shard_map/psum | solution.py:67
  420.3 11.7 cholesky.214
  432.0 9.8 custom-call.17
  442.3 11.7 cholesky.231
  456.3 4.3 while.8
  457.1 1.4 bitcast_dynamic-update-slice_fusion.8
  459.1 1.4 bitcast_dynamic-update-slice_fusion.8
  460.6 19.7 %custom-call.18 = f32[2,128,128]{1,2,0:T(8,128)S(1)} custom-call(f32[2,128,128]{2,1,0:T(8,128)S(1)} %get-tuple-element.30), custom_call_target="InvertDiagBlocksLowerTriangular" | custom-call | tf_op jit(solution)/shard_map/jit(_solve_triangular)/triangular_solve | solution.py:16
  482.4 63.8 %all_to_all.10 = f32[8,640,256]{2,1,0:T(8,128)} all-to-all(f32[8,640,256]{2,1,0:T(8,128)S(1)} %stack.11), channel_id=1, replica_groups=mesh['col'=4,'row'=8] {'row'}, dimensions={0} | all-to-all | bytes 10485760 | tf_op jit(solution)/shard_map/all_to_all | solution.py:51
  546.2 12.1 %gather_fusion.1 = f32[120,128,256]{2,1,0:T(8,128)} fusion(f32[40,128,256]{2,1,0:T(8,128)} %bitcast.162, s32[1024]{0:T(1024)S(1)} %pad_clamp_fusion), kind=kCustom, calls=%fused_computation.1 | custom fusion | bytes 31457760 | tf_op jit(solution)/shard_map/gather | solution.py:54
  558.3 20.2 %convolution_bitcast_fusion = f32[120,128,256]{1,2,0:T(8,128)} fusion(f32[120,128,256]{2,1,0:T(8,128)} %gather_fusion.1, bf16[120,128,128]{2,1,0:T(8,128)(2,1)} %param.8), kind=kOutput, calls=%fused_computation.10 | convolution fusion | flops 6039797760 | bytes 35389440 | tf_op jit(solution)/shard_map/sij,sjk->sik/dot_general | solution.py:55
  578.5 15.7 %copy.42 = f32[15,8,128,256]{3,1,2,0:T(8,128)} copy(f32[15,8,128,256]{2,3,1,0:T(8,128)} %bitcast.166) | data formatting | bytes 31457280
  594.2 11.6 fusion.51
  605.8 76.1 %fusion.1 = f32[8,32768]{1,0:T(8,128)S(1)} fusion(f32[20,32768]{1,0:T(8,128)} %fusion.51), kind=kCustom, calls=%all-reduce-scatter.1 | all-reduce-scatter fusion | flops 1048577 | bytes 3670528
  681.8 3.0 collective-permute-start.2
  684.9 1.6 collective-permute-start.3
  686.6 1.9 fusion.82
  688.5 18.9 %collective-permute-done.3 = f32[1,32768]{1,0:T(1,128)S(1)} collective-permute-done((f32[1,32768]{1,0:T(1,128)S(1)}, f32[1,32768]{1,0:T(1,128)S(1)}, u32[]{:S(2)}, u32[]{:S(2)}) %collective-permute-start.3) | collective-permute-done | bytes 131104
  707.4 21.2 %concatenate.4 = f32[17,32768]{1,0:T(8,128)} concatenate(f32[1,32768]{1,0:T(1,128)S(1)} %collective-permute-done.3, f32[8,32768]{1,0:T(8,128)} %collective-permute-done.2, f32[8,32768]{1,0:T(8,128)S(1)} %fusion.1), dimensions={0} | concatenate | bytes 4456448
  728.6 1.7 constant_dynamic-slice_fusion.4
  730.6 2.1 fusion.30
  732.9 133.0 %all-reduce.15.cloned.1.call-done = (f32[256,256]{0,1:T(8,128)}, f32[256,256]{1,0:T(8,128)}) async-done(((f32[256,256]{0,1:T(8,128)}, f32[256,256]{1,0:T(8,128)}), (f32[256,256]{0,1:T(8,128)}, f32[256,256]{1,0:T(8,128)})) %all-reduce.15.cloned.1.call-update) | async-done | bytes 524304 | tf_op jit(solution)/shard_map/psum | solution.py:70
  868.0 11.7 cholesky.248
  879.7 9.8 custom-call.19
  890.0 11.7 cholesky.265
  904.4 4.0 while.9
  905.0 1.4 bitcast_dynamic-update-slice_fusion.9
  907.0 1.4 bitcast_dynamic-update-slice_fusion.9
  908.4 19.8 %custom-call.20 = f32[2,128,128]{1,2,0:T(8,128)S(1)} custom-call(f32[2,128,128]{2,1,0:T(8,128)S(1)} %get-tuple-element.31), custom_call_target="InvertDiagBlocksLowerTriangular" | custom-call | tf_op jit(solution)/shard_map/jit(_solve_triangular)/triangular_solve | solution.py:16
  931.0 11.7 cholesky.282
  942.7 9.8 custom-call.21
  953.0 11.9 cholesky.299
  967.6 4.0 while.10
  968.2 1.4 bitcast_dynamic-update-slice_fusion.10
  970.2 1.4 bitcast_dynamic-update-slice_fusion.10
  971.6 19.7 %custom-call.22 = f32[2,128,128]{1,2,0:T(8,128)S(1)} custom-call(f32[2,128,128]{2,1,0:T(8,128)S(1)} %get-tuple-element.32), custom_call_target="InvertDiagBlocksLowerTriangular" | custom-call | tf_op jit(solution)/shard_map/jit(_solve_triangular)/triangular_solve | solution.py:16
  992.9 1.9 fusion.83
  996.0 124.6 %all-reduce.13.cloned.1.call-done = f32[256,256]{0,1:T(8,128)} async-done(((f32[256,256]{0,1:T(8,128)}), f32[256,256]{0,1:T(8,128)}) %all-reduce.13.cloned.1.call-update) | async-done | bytes 262160 | tf_op jit(solution)/shard_map/psum | solution.py:85
  1122.7 11.7 cholesky.316
  1134.5 9.8 custom-call.23
  1144.8 11.9 %cholesky.333 = f32[128,128]{1,0:T(8,128)S(1)} custom-call(f32[128,128]{1,0:T(8,128)S(1)} %convolution_subtract_fusion.4), custom_call_target="Cholesky" | custom-call | tf_op jit(solution)/shard_map/jit(cholesky)/cholesky | solution.py:15
  1159.5 4.1 while.11
  1160.2 1.4 bitcast_dynamic-update-slice_fusion.11
  1162.2 1.4 bitcast_dynamic-update-slice_fusion.11
  1163.7 19.7 %custom-call.24 = f32[2,128,128]{1,2,0:T(8,128)S(1)} custom-call(f32[2,128,128]{2,1,0:T(8,128)S(1)} %get-tuple-element.33), custom_call_target="InvertDiagBlocksLowerTriangular" | custom-call | tf_op jit(solution)/shard_map/jit(_solve_triangular)/triangular_solve | solution.py:16
  1184.2 1.6 convolution_multiply_fusion
  (110 shorter events, 29.7 us)
Async XLA Ops:
  38.3 5.0 copy-start.3
  38.3 65.1 %all-to-all-start = ((f32[8,640,256]{2,1,0:T(8,128)}), f32[8,640,256]{2,1,0:T(8,128)}, u32[]{:S(2)}, u32[]{:S(2)}) async-start(f32[8,640,256]{2,1,0:T(8,128)} %stack.10), calls=%async_computation | async-start | bytes 10485760 | tf_op jit(solution)/shard_map/all_to_all | solution.py:51
  43.1 375.1 %all-reduce.11.cloned.1.call-start = ((), (), s32[]{:S(2)}) async-start(), calls=%async_computation.2 | async-start | bytes 524288 | tf_op jit(solution)/shard_map/psum | solution.py:67
  135.7 15.7 %copy-start.2 = (s32[120]{0:T(128)S(1)}, s32[120]{0:T(128)}, u32[]{:S(2)}) copy-start(s32[120]{0:T(128)} %param.9) | copy-start | bytes 1444
  234.8 46.6 %copy-start = (f32[640,256]{1,0:T(8,128)S(1)}, f32[640,256]{1,0:T(8,128)}, u32[]{:S(2)}) copy-start(f32[640,256]{1,0:T(8,128)} %param.12) | copy-start | bytes 1966084
  234.8 23.3 %collective-permute-start = (f32[8,32768]{1,0:T(8,128)}, f32[8,32768]{1,0:T(8,128)S(1)}, u32[]{:S(2)}, u32[]{:S(2)}) collective-permute-start(f32[8,32768]{1,0:T(8,128)} %fusion), channel_id=1, source_target_pairs={{0,8},{8,16},{16,24},{1,9},{9,17},{17,25},{2,10},{10,18},{18,26},{... | collective-permute-start | bytes 3145736
  237.6 20.5 %collective-permute-start.1 = (f32[1,32768]{1,0:T(1,128)S(1)}, f32[1,32768]{1,0:T(1,128)S(1)}, u32[]{:S(2)}, u32[]{:S(2)}) collective-permute-start(f32[1,32768]{1,0:T(1,128)S(1)} %slice.54), channel_id=1, source_target_pairs={{0,16},{8,24},{1,17},{9,25},{2,18},{10,26},{3,19},{11,27},{4,20},{... | collective-permute-start | bytes 393224
  283.6 582.3 %all-reduce.15.cloned.1.call-start = ((), (), s32[]{:S(2)}) async-start(), calls=%async_computation.4 | async-start | bytes 1048576 | tf_op jit(solution)/shard_map/psum | solution.py:70
  681.8 25.6 %collective-permute-start.2 = (f32[8,32768]{1,0:T(8,128)S(1)}, f32[8,32768]{1,0:T(8,128)}, u32[]{:S(2)}, u32[]{:S(2)}) collective-permute-start(f32[8,32768]{1,0:T(8,128)S(1)} %fusion.1), channel_id=1, source_target_pairs={{0,8},{8,16},{16,24},{1,9},{9,17},{17,25},{2,10},{10,18},{18,26},{... | collective-permute-start | bytes 3145736
  684.9 22.4 %collective-permute-start.3 = (f32[1,32768]{1,0:T(1,128)S(1)}, f32[1,32768]{1,0:T(1,128)S(1)}, u32[]{:S(2)}, u32[]{:S(2)}) collective-permute-start(f32[1,32768]{1,0:T(1,128)S(1)} %slice.55), channel_id=1, source_target_pairs={{0,16},{8,24},{1,17},{9,25},{2,18},{10,26},{3,19},{11,27},{4,20},{... | collective-permute-start | bytes 393224
  732.8 387.9 %all-reduce.13.cloned.1.call-start = ((), (), s32[]{:S(2)}) async-start(), calls=%async_computation.3 | async-start | bytes 524288 | tf_op jit(solution)/shard_map/psum | solution.py:85
  865.8 64.1 %copy-start.1 = (f32[256,256]{1,0:T(8,128)S(1)}, f32[256,256]{1,0:T(8,128)}, u32[]{:S(2)}) copy-start(f32[256,256]{1,0:T(8,128)} %get-tuple-element.67) | copy-start | bytes 786436
Sparse Core Ops, SparseCore 0:
  283.7 134.4 all-reduce.10
  732.9 132.8 all-reduce.14
  995.0 125.6 all-reduce.12
